TPU v7x, 256 devices: a whole 4x4x8 slice. The times are simulated.
256 devices in a mesh: row: 16 (over x_lo, z), col: 16 (over x_hi, y, core).
Axes of the slice: x: 4 (x_hi: 2, x_lo: 2; x = x_hi * 2 + x_lo), y: 4, z: 8, core: 2. Of those that a mesh axis runs over, the one named last changes fastest.
Arguments:
- features: bfloat16 [32768, 1024], P(('row', 'col')), may hold values from -6 to 6
- weight: bfloat16 [1024, 1024], replicated, may hold values from -0.1875 to 0.1875
- cotangent: bfloat16 [32768, 1024], P(('col', 'row')), may hold values from -6 to 6
- tile_values: bfloat16 [16, 16, 64, 128, 128], P('row', 'col'), may hold values from -0.1875 to 0.1875
- block_row: int32 [16, 16, 64], P('row', 'col'), may hold values from 0 to 15, as said below
- block_column: int32 [16, 16, 64], P('row', 'col'), may hold values from 0 to 15, as said below
- tile_count: int32 [16, 16], P('row', 'col'), may hold values from 16 to 64, as said below
Outputs:
- activated: bfloat16 [32768, 1024], P(('col', 'row'))
- feat_grad: bfloat16 [32768, 1024], P(('row', 'col'))
- weight_grad: float32 [1024, 1024], replicated
Inputs may be any that keep to these rules, and one draw needn't show every extreme that they name: `block_row`: within one grid position the slots name distinct region cells. `block_column`: within one grid position the slots name distinct region cells. `tile_count`: some grid position has exactly 64 live slots.
All inputs are finite; a program needn't handle non-finite values.
Results may differ from a plain program's by a relative error of at most 0.02.
Values may be sent and summed in bfloat16 or wider, within the bound.
A program may use at most 128 MiB of HBM per device.

v0:
```python
import jax
import jax.numpy as jnp
from jax import lax
from jax.sharding import PartitionSpec as P


def silu_slope(hidden):
    sigmoid = jax.nn.sigmoid(hidden)
    return sigmoid * (1.0 + hidden * (1.0 - sigmoid))


def spread_tiles(source, tile_block, index_in, index_out, live_count, out_blocks, flipped):
    block_size = tile_block.shape[-1]
    width = source.shape[-1]
    blocks = source.reshape(-1, block_size, width)
    per_turn = 16
    form = "tba,tbf->taf" if flipped else "tab,tbf->taf"

    def add_turn(turn, summed):
        first = turn * per_turn
        matrix = lax.dynamic_slice_in_dim(tile_block, first, per_turn, 0)
        wanted = lax.dynamic_slice_in_dim(index_in, first, per_turn, 0)
        placed = lax.dynamic_slice_in_dim(index_out, first, per_turn, 0)
        is_live = first + jnp.arange(per_turn, dtype=jnp.int32) < live_count
        picked = blocks[wanted]
        products = jnp.einsum(form, matrix, picked, preferred_element_type=jnp.float32)
        products = products * is_live.astype(jnp.float32)[:, None, None]
        return summed.at[placed].add(products)

    turns = (live_count + per_turn - 1) // per_turn
    summed = lax.fori_loop(
        0, turns, add_turn, jnp.zeros((out_blocks, block_size, width), jnp.float32)
    )
    return summed.reshape(out_blocks * block_size, width)


def on_device(features, weight, cotangent, tile_values, block_row, block_column, tile_count):
    row_devices = lax.axis_size("row")
    col_devices = lax.axis_size("col")
    span = features.shape[0]
    block_size = tile_values.shape[-1]
    per_device = span // block_size
    tile_block = tile_values[0, 0]
    rows_index = block_row[0, 0]
    cols_index = block_column[0, 0]
    live_count = tile_count[0, 0]
    projected = jnp.dot(features, weight, preferred_element_type=jnp.float32).astype(jnp.bfloat16)
    gathered = lax.all_gather(projected, "col", axis=0, tiled=True)
    partial_value = spread_tiles(
        gathered, tile_block, cols_index, rows_index, live_count, row_devices * per_device, False
    )
    hidden = lax.psum_scatter(
        partial_value.astype(jnp.bfloat16), "row", scatter_dimension=0, tiled=True
    ).astype(jnp.float32)
    activated = jax.nn.silu(hidden).astype(jnp.bfloat16)
    hidden_grad = (cotangent.astype(jnp.float32) * silu_slope(hidden)).astype(jnp.bfloat16)
    grad_group = lax.all_gather(hidden_grad, "row", axis=0, tiled=True)
    back_partial = spread_tiles(
        grad_group, tile_block, rows_index, cols_index, live_count, col_devices * per_device, True
    )
    feat_delta = lax.psum_scatter(
        back_partial.astype(jnp.bfloat16), "col", scatter_dimension=0, tiled=True
    )
    feat_grad = jnp.dot(feat_delta, weight.T, preferred_element_type=jnp.float32).astype(
        jnp.bfloat16
    )
    weight_terms = lax.dot_general(
        features, feat_delta, (((0,), (0,)), ((), ())), preferred_element_type=jnp.float32
    )
    factor = (span * row_devices * col_devices) ** (-0.5)
    weight_grad = lax.psum(weight_terms, ("row", "col")) * factor
    return (activated, feat_grad, weight_grad)


def solution(mesh):
    return jax.shard_map(
        on_device,
        mesh=mesh,
        in_specs=(
            P(("row", "col"), None),
            P(),
            P(("col", "row"), None),
            P("row", "col", None, None, None),
            P("row", "col", None),
            P("row", "col", None),
            P("row", "col"),
        ),
        out_specs=(P(("col", "row"), None), P(("row", "col"), None), P()),
        check_vma=False,
    )
```

profile of v0, /device:TPU:2, one launch (start us, length us, event | category | flops | bytes accessed | tf_op | source)
XLA Modules:
  0.0 871.9 jit_solution(16505086763936700742)
XLA Ops:
  7.2 1.5 copy-done
  8.8 2.1 convolution_convert_fusion.1
  11.6 61.6 %all-gather.3.cloned.1.call-done = bf16[2048,1024]{1,0:T(8,128)(2,1)} async-done(((bf16[128,1024]{1,0:T(8,128)(2,1)}), bf16[2048,1024]{1,0:T(8,128)(2,1)}) %all-gather.3.cloned.1.call-update) | async-done | bytes 4194320 | tf_op jit(solution)/shard_map/all_gather | solution.py:48
  73.2 4.3 broadcast.35.clone
  77.6 30.5 %while.20 = (s32[]{:T(128)}, f32[16,128,1024]{2,1,0:T(8,128)}, s32[]{:T(128)}, s32[64]{0:T(128)S(1)}, bf16[64,128,128]{2,1,0:T(8,128)(2,1)}, /*index=5*/s32[64]{...) while((s32[]{:T(128)}, f32[16,128,1024]{2,1,0:T(8,128)}, ...), condition=%wide.region_2.3_spmd, body=%wide.region_0.2_spmd.sunk | while | flops 541066368 | bytes 46666480 | solution.py:31
  77.6 0.6 compare_convert_fusion.4
  78.2 0.1 compare_select_fusion.6
  78.3 5.0 gather_fusion
  83.3 6.8 broadcast_multiply_fusion.5
  90.1 17.9 %scatter_fusion = f32[16,128,1024]{2,1,0:T(8,128)} fusion(f32[16,128,1024]{2,1,0:T(8,128)} %get-tuple-element.261, s32[16]{0:T(128)S(1)} %get-tuple-element.236, f32[16,128,1024]{2,1,0:T(8,128)} %broadcast_multiply_fusion.5), kind=kCustom, calls=%fused_computation.2.clone.1 | custom fusion | flops 2097152 | bytes 25165888 | tf_op jit(solution)/shard_map/while/body/scatter-add | solution.py:28
  108.0 6.1 convert_element_type.45
  114.1 0.0 all-gather.5.cloned.1.call-start
  114.2 171.5 %reduce-scatter.3.cloned.1.call-done = bf16[128,1024]{1,0:T(8,128)(2,1)} async-done(((bf16[2048,1024]{1,0:T(8,128)(2,1)}), bf16[128,1024]{1,0:T(8,128)(2,1)}) %reduce-scatter.3.cloned.1.call-update) | async-done | bytes 262160 | tf_op jit(solution)/shard_map/reduce_scatter | solution.py:52
  285.6 2.0 fusion.11
  287.7 0.0 reduce-scatter.5.cloned.1.call-start
  287.7 4.1 copy.10
  291.8 68.7 %all-gather.5.cloned.1.call-done = bf16[2048,1024]{1,0:T(8,128)(2,1)} async-done(((bf16[128,1024]{1,0:T(8,128)(2,1)}), bf16[2048,1024]{1,0:T(8,128)(2,1)}) %all-gather.5.cloned.1.call-update) | async-done | bytes 4194320 | tf_op jit(solution)/shard_map/all_gather | solution.py:57
  360.5 4.3 broadcast.35
  364.7 30.7 %while.21 = (s32[]{:T(128)}, f32[16,128,1024]{2,1,0:T(8,128)}, s32[]{:T(128)}, s32[64]{0:T(128)S(1)}, bf16[64,128,128]{1,2,0:T(8,128)(2,1)}, /*index=5*/s32[64]{...) while((s32[]{:T(128)}, f32[16,128,1024]{2,1,0:T(8,128)}, ...), condition=%wide.region_6.7_spmd, body=%wide.region_4.6_spmd.sunk | while | flops 541066368 | bytes 46666480 | solution.py:31
  364.7 0.6 compare_convert_fusion.5
  365.4 0.1 compare_select_fusion.7
  365.5 5.0 gather_fusion.1
  370.5 6.8 broadcast_multiply_fusion.6
  377.3 18.1 %scatter_fusion.1 = f32[16,128,1024]{2,1,0:T(8,128)} fusion(f32[16,128,1024]{2,1,0:T(8,128)} %get-tuple-element.297, s32[16]{0:T(128)S(1)} %get-tuple-element.246, f32[16,128,1024]{2,1,0:T(8,128)} %broadcast_multiply_fusion.6), kind=kCustom, calls=%fused_computation.3.clone.1 | custom fusion | flops 2097152 | bytes 25165888 | tf_op jit(solution)/shard_map/while/body/scatter-add | solution.py:28
  395.4 6.1 convert_element_type.51
  401.5 0.0 all-reduce.2.cloned.1.call-start
  401.5 177.7 %reduce-scatter.5.cloned.1.call-done = bf16[128,1024]{1,0:T(8,128)(2,1)} async-done(((bf16[2048,1024]{1,0:T(8,128)(2,1)}), bf16[128,1024]{1,0:T(8,128)(2,1)}) %reduce-scatter.5.cloned.1.call-update) | async-done | bytes 262160 | tf_op jit(solution)/shard_map/reduce_scatter | solution.py:61
  579.2 3.8 convolution_bitcast_fusion
  583.0 1.5 convolution_convert_fusion
  584.6 270.4 %all-reduce.2.cloned.1.call-done = f32[1024,1024]{0,1:T(8,128)} async-done(((f32[1024,1024]{0,1:T(8,128)}), f32[1024,1024]{0,1:T(8,128)}) %all-reduce.2.cloned.1.call-update) | async-done | bytes 4194320 | tf_op jit(solution)/shard_map/psum | solution.py:71
  855.0 5.1 broadcast_multiply_fusion.2
  860.1 5.3 copy.12
  (20 shorter events, 0.2 us)
Async XLA Ops:
  7.2 1.6 copy-start
  7.2 66.1 %all-gather.3.cloned.1.call-start = ((), (), s32[]{:S(2)}) async-start(), calls=%async_computation.2 | async-start | bytes 4456448 | tf_op jit(solution)/shard_map/all_gather | solution.py:48
  10.9 274.8 %reduce-scatter.3.cloned.1.call-start = ((), (), s32[]{:S(2)}) async-start(), calls=%async_computation.3 | async-start | bytes 4456448 | tf_op jit(solution)/shard_map/reduce_scatter | solution.py:52
  73.2 4.3 copy-start.4
  73.2 4.3 copy-start.5
  114.1 171.6 %copy-start.3 = (bf16[128,1024]{1,0:T(8,128)(2,1)S(1)}, bf16[128,1024]{1,0:T(8,128)(2,1)}, u32[]{:S(2)}) copy-start(bf16[128,1024]{1,0:T(8,128)(2,1)} %param.13) | copy-start | bytes 786436
  114.1 246.4 %all-gather.5.cloned.1.call-start = ((), (), s32[]{:S(2)}) async-start(), calls=%async_computation.4 | async-start | bytes 4456448 | tf_op jit(solution)/shard_map/all_gather | solution.py:57
  287.7 291.6 %reduce-scatter.5.cloned.1.call-start = ((), (), s32[]{:S(2)}) async-start(), calls=%async_computation.5 | async-start | bytes 4456448 | tf_op jit(solution)/shard_map/reduce_scatter | solution.py:61
  401.5 177.8 %copy-start.1 = (bf16[128,1024]{1,0:T(8,128)(2,1)S(1)}, bf16[128,1024]{1,0:T(8,128)(2,1)}, u32[]{:S(2)}) copy-start(bf16[128,1024]{1,0:T(8,128)(2,1)} %param.11) | copy-start | bytes 786436
  401.5 453.5 %all-reduce.2.cloned.1.call-start = ((), (), s32[]{:S(2)}) async-start(), calls=%async_computation.6 | async-start | bytes 8388608 | tf_op jit(solution)/shard_map/psum | solution.py:71
  579.2 3.8 copy-start.2
Sparse Core Ops, SparseCore 0:
  11.3 61.8 all-gather.2
  114.2 171.3 reduce-scatter.2
  288.0 72.3 all-gather.4
  401.6 177.5 reduce-scatter.4
  585.1 269.8 all-reduce.1
where the time goes:
time: 873 us; the launch traced here: 872 us
  waiting for transfers between devices  750 us (86%)
  other arithmetic  56.6 us (6%)
  local copies, waits for them, and re-layouts  29.6 us (3%)
  matrix products  21 us (2%)
  between operations  14.5 us (2%)
    psum x1, waiting for transfers between devices, on_device(): weight_grad = lax.psum(weight_terms, ('row', 'col')) * factor  270 us
    reduce_scatter x1, waiting for transfers between devices, on_device(): lax.psum_scatter(back_partial.astype(jnp.bfloat16), 'col', scatter_dimens...  178 us
    reduce_scatter x1, waiting for transfers between devices, on_device(): lax.psum_scatter(partial_value.astype(jnp.bfloat16), 'row', scatter_dimen...  171 us
    all_gather x1, waiting for transfers between devices, on_device(): grad_group = lax.all_gather(hidden_grad, 'row', axis=0, tiled=True)  68.7 us
    all_gather x1, waiting for transfers between devices, on_device(): gathered = lax.all_gather(projected, 'col', axis=0, tiled=True)  61.6 us
    scatter-add x2, other arithmetic, add_turn(): return summed.at[placed].add(products)  35.9 us
  transfers between devices with their start and end apart: 5, of which 5 were waited for; matrix products, arithmetic and copies ran while one was open for 1% of the time, Pallas kernels for 0%

commit v1 on v0

--- a/solution.py
+++ b/solution.py
@@ -2,6 +2,11 @@
 import jax.numpy as jnp
 from jax import lax
 from jax.sharding import PartitionSpec as P
+
+
+def axis_by_axis(array, axis_one, axis_two):
+    half = lax.psum(array, axis_one)
+    return lax.psum(half, axis_two)
 
 
 def silu_slope(hidden):
@@ -68,7 +73,7 @@
         features, feat_delta, (((0,), (0,)), ((), ())), preferred_element_type=jnp.float32
     )
     factor = (span * row_devices * col_devices) ** (-0.5)
-    weight_grad = lax.psum(weight_terms, ("row", "col")) * factor
+    weight_grad = axis_by_axis(weight_terms, "row", "col") * factor
     return (activated, feat_grad, weight_grad)
 
 

time: 873 us -> 911 us (1.044)
  waiting for transfers between devices: 750 us -> 786 us
    psum x1 -> x2, waiting for transfers between devices: 270 us -> 307 us  [the longest x1 153 us: axis_by_axis(): half = lax.psum(array, axis_one)]
  transfers between devices with their start and end apart: 5 -> 6, of which waited for: 5 -> 6; matrix products, arithmetic and copies ran while one was open for 1% -> 1% of each run, Pallas kernels for 0% -> 0%
where the time goes in v1:
time: 911 us; the launch traced here: 909 us
  waiting for transfers between devices  786 us (86%)
  other arithmetic  56.6 us (6%)
  local copies, waits for them, and re-layouts  29.6 us (3%)
  matrix products  21 us (2%)
  between operations  14.8 us (2%)
    reduce_scatter x1, waiting for transfers between devices, on_device(): lax.psum_scatter(back_partial.astype(jnp.bfloat16), 'col', scatter_dimens...  178 us
    reduce_scatter x1, waiting for transfers between devices, on_device(): lax.psum_scatter(partial_value.astype(jnp.bfloat16), 'row', scatter_dimen...  171 us
    psum x1, waiting for transfers between devices, axis_by_axis(): half = lax.psum(array, axis_one)  153 us
    psum x1, waiting for transfers between devices, axis_by_axis(): return lax.psum(half, axis_two)  153 us
    all_gather x1, waiting for transfers between devices, on_device(): grad_group = lax.all_gather(hidden_grad, 'row', axis=0, tiled=True)  68.7 us
    all_gather x1, waiting for transfers between devices, on_device(): gathered = lax.all_gather(projected, 'col', axis=0, tiled=True)  61.6 us
    scatter-add x2, other arithmetic, add_turn(): return summed.at[placed].add(products)  35.9 us
  transfers between devices with their start and end apart: 6, of which 6 were waited for; matrix products, arithmetic and copies ran while one was open for 1% of the time, Pallas kernels for 0%

profile of v1, /device:TPU:2, one launch (start us, length us, event | category | flops | bytes accessed | tf_op | source)
XLA Modules:
  0.0 908.7 jit_solution(16452895451050484518)
XLA Ops:
  7.2 1.5 copy-done
  8.8 2.1 convolution_convert_fusion.1
  11.6 61.6 %all-gather.3.cloned.1.call-done = bf16[2048,1024]{1,0:T(8,128)(2,1)} async-done(((bf16[128,1024]{1,0:T(8,128)(2,1)}), bf16[2048,1024]{1,0:T(8,128)(2,1)}) %all-gather.3.cloned.1.call-update) | async-done | bytes 4194320 | tf_op jit(solution)/shard_map/all_gather | solution.py:53
  73.2 4.3 broadcast.35.clone
  77.6 30.5 %while.20 = (s32[]{:T(128)}, f32[16,128,1024]{2,1,0:T(8,128)}, s32[]{:T(128)}, s32[64]{0:T(128)S(1)}, bf16[64,128,128]{2,1,0:T(8,128)(2,1)}, /*index=5*/s32[64]{...) while((s32[]{:T(128)}, f32[16,128,1024]{2,1,0:T(8,128)}, ...), condition=%wide.region_2.3_spmd, body=%wide.region_0.2_spmd.sunk | while | flops 541066368 | bytes 46666480 | solution.py:36
  77.6 0.6 compare_convert_fusion.4
  78.2 0.1 compare_select_fusion.6
  78.3 5.0 gather_fusion
  83.3 6.8 broadcast_multiply_fusion.5
  90.1 17.9 %scatter_fusion = f32[16,128,1024]{2,1,0:T(8,128)} fusion(f32[16,128,1024]{2,1,0:T(8,128)} %get-tuple-element.261, s32[16]{0:T(128)S(1)} %get-tuple-element.236, f32[16,128,1024]{2,1,0:T(8,128)} %broadcast_multiply_fusion.5), kind=kCustom, calls=%fused_computation.2.clone.1 | custom fusion | flops 2097152 | bytes 25165888 | tf_op jit(solution)/shard_map/while/body/scatter-add | solution.py:33
  108.0 6.1 convert_element_type.45
  114.2 171.5 %reduce-scatter.3.cloned.1.call-done = bf16[128,1024]{1,0:T(8,128)(2,1)} async-done(((bf16[2048,1024]{1,0:T(8,128)(2,1)}), bf16[128,1024]{1,0:T(8,128)(2,1)}) %reduce-scatter.3.cloned.1.call-update) | async-done | bytes 262160 | tf_op jit(solution)/shard_map/reduce_scatter | solution.py:57
  285.6 2.0 fusion.11
  287.7 0.0 reduce-scatter.5.cloned.1.call-start
  287.7 4.1 copy.10
  291.8 68.7 %all-gather.5.cloned.1.call-done = bf16[2048,1024]{1,0:T(8,128)(2,1)} async-done(((bf16[128,1024]{1,0:T(8,128)(2,1)}), bf16[2048,1024]{1,0:T(8,128)(2,1)}) %all-gather.5.cloned.1.call-update) | async-done | bytes 4194320 | tf_op jit(solution)/shard_map/all_gather | solution.py:62
  360.5 4.3 broadcast.35
  364.7 30.7 %while.21 = (s32[]{:T(128)}, f32[16,128,1024]{2,1,0:T(8,128)}, s32[]{:T(128)}, s32[64]{0:T(128)S(1)}, bf16[64,128,128]{1,2,0:T(8,128)(2,1)}, /*index=5*/s32[64]{...) while((s32[]{:T(128)}, f32[16,128,1024]{2,1,0:T(8,128)}, ...), condition=%wide.region_6.7_spmd, body=%wide.region_4.6_spmd.sunk | while | flops 541066368 | bytes 46666480 | solution.py:36
  364.7 0.6 compare_convert_fusion.5
  365.4 0.1 compare_select_fusion.7
  365.5 5.0 gather_fusion.1
  370.5 6.8 broadcast_multiply_fusion.6
  377.3 18.1 %scatter_fusion.1 = f32[16,128,1024]{2,1,0:T(8,128)} fusion(f32[16,128,1024]{2,1,0:T(8,128)} %get-tuple-element.297, s32[16]{0:T(128)S(1)} %get-tuple-element.246, f32[16,128,1024]{2,1,0:T(8,128)} %broadcast_multiply_fusion.6), kind=kCustom, calls=%fused_computation.3.clone.1 | custom fusion | flops 2097152 | bytes 25165888 | tf_op jit(solution)/shard_map/while/body/scatter-add | solution.py:33
  395.4 6.1 convert_element_type.51
  401.5 0.0 all-reduce.3.cloned.1.call-start
  401.5 177.7 %reduce-scatter.5.cloned.1.call-done = bf16[128,1024]{1,0:T(8,128)(2,1)} async-done(((bf16[2048,1024]{1,0:T(8,128)(2,1)}), bf16[128,1024]{1,0:T(8,128)(2,1)}) %reduce-scatter.5.cloned.1.call-update) | async-done | bytes 262160 | tf_op jit(solution)/shard_map/reduce_scatter | solution.py:66
  579.2 3.7 convolution_bitcast_fusion
  583.0 153.5 %all-reduce.3.cloned.1.call-done = f32[1024,1024]{0,1:T(8,128)} async-done(((f32[1024,1024]{0,1:T(8,128)}), f32[1024,1024]{0,1:T(8,128)}) %all-reduce.3.cloned.1.call-update) | async-done | bytes 4194320 | tf_op jit(solution)/shard_map/psum | solution.py:8
  736.5 1.5 convolution_convert_fusion
  738.1 153.4 %all-reduce.5.cloned.1.call-done = f32[1024,1024]{0,1:T(8,128)} async-done(((f32[1024,1024]{0,1:T(8,128)}), f32[1024,1024]{0,1:T(8,128)}) %all-reduce.5.cloned.1.call-update) | async-done | bytes 4194320 | tf_op jit(solution)/shard_map/psum | solution.py:9
  891.4 5.1 broadcast_multiply_fusion.2
  896.5 5.3 copy.12
  (23 shorter events, 0.3 us)
Async XLA Ops:
  7.2 1.6 copy-start
  7.2 66.1 %all-gather.3.cloned.1.call-start = ((), (), s32[]{:S(2)}) async-start(), calls=%async_computation.2 | async-start | bytes 4456448 | tf_op jit(solution)/shard_map/all_gather | solution.py:53
  10.9 274.8 %reduce-scatter.3.cloned.1.call-start = ((), (), s32[]{:S(2)}) async-start(), calls=%async_computation.3 | async-start | bytes 4456448 | tf_op jit(solution)/shard_map/reduce_scatter | solution.py:57
  73.2 4.3 copy-start.4
  73.2 4.3 copy-start.5
  114.1 171.6 %copy-start.3 = (bf16[128,1024]{1,0:T(8,128)(2,1)S(1)}, bf16[128,1024]{1,0:T(8,128)(2,1)}, u32[]{:S(2)}) copy-start(bf16[128,1024]{1,0:T(8,128)(2,1)} %param.13) | copy-start | bytes 786436
  114.1 246.4 %all-gather.5.cloned.1.call-start = ((), (), s32[]{:S(2)}) async-start(), calls=%async_computation.4 | async-start | bytes 4456448 | tf_op jit(solution)/shard_map/all_gather | solution.py:62
  287.7 291.6 %reduce-scatter.5.cloned.1.call-start = ((), (), s32[]{:S(2)}) async-start(), calls=%async_computation.5 | async-start | bytes 4456448 | tf_op jit(solution)/shard_map/reduce_scatter | solution.py:66
  401.5 177.8 %copy-start.1 = (bf16[128,1024]{1,0:T(8,128)(2,1)S(1)}, bf16[128,1024]{1,0:T(8,128)(2,1)}, u32[]{:S(2)}) copy-start(bf16[128,1024]{1,0:T(8,128)(2,1)} %param.11) | copy-start | bytes 786436
  401.5 335.0 %all-reduce.3.cloned.1.call-start = ((), (), s32[]{:S(2)}) async-start(), calls=%async_computation.6 | async-start | bytes 8388608 | tf_op jit(solution)/shard_map/psum | solution.py:8
  582.9 153.6 %copy-start.2 = (bf16[128,1024]{1,0:T(8,128)(2,1)S(1)}, bf16[128,1024]{1,0:T(8,128)(2,1)}, u32[]{:S(2)}) copy-start(bf16[128,1024]{1,0:T(8,128)(2,1)} %reduce-scatter.5.cloned.1.call-done) | copy-start | bytes 786436
  582.9 308.5 %all-reduce.5.cloned.1.call-start = ((), (), s32[]{:S(2)}) async-start(), calls=%async_computation.7 | async-start | bytes 8388608 | tf_op jit(solution)/shard_map/psum | solution.py:9
Sparse Core Ops, SparseCore 0:
  11.3 61.8 all-gather.2
  114.2 171.3 reduce-scatter.2
  288.0 72.3 all-gather.4
  401.6 177.5 reduce-scatter.4
  583.1 153.3 all-reduce.2
  739.0 152.3 all-reduce.4
